TPU v7x, 512 devices: a whole 4x4x16 slice. The times are simulated.
512 devices in a mesh: space: 64 (over z, x_hi, core), scen: 8 (over x_lo, y).
Axes of the slice: x: 4 (x_hi: 2, x_lo: 2; x = x_hi * 2 + x_lo), y: 4, z: 16, core: 2. Of those that a mesh axis runs over, the one named last changes fastest.
Arguments:
- dwell_map: bfloat16 [16384, 1024], P('space', 'scen'), may hold values from 0 to 1
- target_map: bfloat16 [16384, 1024], P('space'), may hold values from -6 to 6
- bound_mask: int32 [16384, 1024], P('space', 'scen'), may hold values 0 or 1
- offsets: int32 [16, 2], replicated, may hold values from -32 to 32, as said below
- rate_index: int32 [16, 1], replicated, may hold values from 0 to 3
- rate_table: float32 [4], replicated, may hold values from 0.5 to 2
- row_kernels: bfloat16 [4, 63], replicated, may hold values from -0.75 to 0.75
- col_kernels: bfloat16 [4, 63], replicated, may hold values from -0.75 to 0.75
Outputs:
- dwell_next: bfloat16 [16384, 1024], P('space', 'scen')
Inputs may be any that keep to these rules, and one draw needn't show every extreme that they name: `offsets`: each entry lies between -32 and 32; in each column some scenario has 32 and another -32. `rate_index`: every level is used by some scenario.
All inputs are finite; a program needn't handle non-finite values. No bound on the sum of `bound_mask` on one device may be relied on, other than what follows from the above.
Results may differ from a plain program's by a relative error of at most 0.014.
Values may be sent and summed in bfloat16 or wider, within the bound.
A program may use at most 64 MiB of HBM per device.

v0:
```python
import jax
import jax.numpy as jnp
from jax import lax
from jax.sharding import PartitionSpec as P

S_DEV = 2
KTAPS = 63
REACH = 32
step_size = 1.0


def extended(x, sides, width):
    for axis, dim in sides:
        count, length = (lax.axis_size(axis), x.shape[dim])
        up = [(i, (i + 1) % count) for i in range(count - 1)]
        down = [(j, i) for i, j in up]
        last = lax.slice_in_dim(x, length - width, length, axis=dim)
        first = lax.slice_in_dim(x, 0, width, axis=dim)
        before = lax.ppermute(last, axis, up)
        after = lax.ppermute(first, axis, down)
        x = jnp.concatenate([before, x, after], axis=dim)
    return x


def band_line(kernel, start_at, row_count, col_count):
    kernel_line = jnp.zeros((col_count + 1,), kernel.dtype)
    kernel_line = lax.dynamic_update_slice(kernel_line, kernel, (start_at,))
    return jnp.tile(kernel_line, row_count)[: row_count * col_count].reshape(row_count, col_count)


def column_pass(values, kernels, shifts):
    scen_count, height, col_total = values.shape
    col_block = 128
    padded = jnp.pad(values, ((0, 0), (0, 0), (col_block, col_block)))

    def column_one_band(kernel, shift):
        return band_line(kernel, shift + col_block, col_block, 3 * col_block)

    matrices = jax.vmap(column_one_band)(kernels, shifts)
    product = jnp.zeros((scen_count, height, col_total // col_block, col_block), jnp.float32)
    for piece in range(3):
        view = padded[:, :, piece * col_block : piece * col_block + col_total].reshape(
            scen_count, height, col_total // col_block, col_block
        )
        part_mat = matrices[:, :, piece * col_block : (piece + 1) * col_block]
        product = product + jnp.einsum(
            "srny,scy->srnc", view, part_mat, preferred_element_type=jnp.float32
        )
    return product.reshape(scen_count, height, col_total)


def row_pass(values, kernels, shifts, out_rows):
    in_rows = values.shape[-2]
    rim_depth = (in_rows - out_rows) // 2
    row_block = 128
    block_count = -(-out_rows // row_block)
    window = row_block + 2 * rim_depth
    if values.ndim == 2:
        padded = values
    else:
        padded = values

    def row_one_band(kernel, shift):
        return band_line(kernel, shift + rim_depth, row_block, window)

    matrices = jax.vmap(row_one_band)(kernels, shifts)
    results = []
    for block_id in range(block_count):
        begin = block_id * row_block
        if values.ndim == 2:
            view = padded[begin : begin + window]
            results.append(
                jnp.einsum("sie,ew->siw", matrices, view, preferred_element_type=jnp.float32)
            )
        else:
            view = padded[:, begin : begin + window]
            results.append(
                jnp.einsum("sie,sew->siw", matrices, view, preferred_element_type=jnp.float32)
            )
    return jnp.concatenate(results, axis=1)


def shards(
    dwell_map, target_map, bound_mask, offsets, rate_index, rate_table, row_kernels, col_kernels
):
    tile_rows = dwell_map.shape[0]
    radius = (KTAPS - 1) // 2
    halo_rows = REACH + radius
    scen_count = S_DEV * lax.axis_size("scen")
    first_scen = lax.axis_index("scen") * S_DEV
    my_offsets = lax.dynamic_slice_in_dim(offsets, first_scen, S_DEV, 0)
    shift_rows = my_offsets[:, 0]
    shift_cols = my_offsets[:, 1]
    level_ids = lax.dynamic_slice_in_dim(rate_index, first_scen, S_DEV, 0)[:, 0]
    onehot = (
        level_ids[:, None] == jnp.arange(rate_table.shape[0], dtype=jnp.int32)[None, :]
    ).astype(jnp.float32)
    my_rates = jnp.sum(onehot * rate_table[None, :], axis=1)
    my_row_taps = jnp.sum(
        onehot[:, :, None] * row_kernels.astype(jnp.float32)[None], axis=1
    ).astype(jnp.bfloat16)
    my_col_taps = jnp.sum(
        onehot[:, :, None] * col_kernels.astype(jnp.float32)[None], axis=1
    ).astype(jnp.bfloat16)
    full_map = lax.all_gather(dwell_map, "scen", axis=1, tiled=True)
    rim_rows = extended(full_map, (("space", 0),), halo_rows)
    forward = row_pass(rim_rows, my_row_taps, -radius - shift_rows, tile_rows).astype(jnp.bfloat16)
    removal = my_rates[:, None, None] * column_pass(forward, my_col_taps, -radius - shift_cols)
    misfit = (removal - target_map.astype(jnp.float32)[None]).astype(jnp.bfloat16)
    misfit_rows = extended(misfit, (("space", 1),), halo_rows)
    back_cols = column_pass(misfit_rows, my_col_taps[:, ::-1], -radius + shift_cols).astype(
        jnp.bfloat16
    )
    adjoint = row_pass(back_cols, my_row_taps[:, ::-1], -radius + shift_rows, tile_rows)
    group_sum = jnp.sum((my_rates / scen_count)[:, None, None] * adjoint, axis=0)
    gradient = lax.psum_scatter(
        group_sum.astype(jnp.bfloat16), "scen", scatter_dimension=1, tiled=True
    ).astype(jnp.float32)
    stepped = dwell_map.astype(jnp.float32) - step_size * gradient
    return jnp.where(bound_mask == 1, jnp.maximum(stepped, 0.0), stepped).astype(jnp.bfloat16)


def solution(mesh):
    return jax.shard_map(
        shards,
        mesh=mesh,
        in_specs=(
            P("space", "scen"),
            P("space", None),
            P("space", "scen"),
            P(),
            P(),
            P(),
            P(),
            P(),
        ),
        out_specs=P("space", "scen"),
        check_vma=False,
    )
```

profile of v0, /device:TPU:32, one launch (start us, length us, event | category | flops | bytes accessed | tf_op | source)
XLA Modules:
  0.0 196.9 jit_solution(3160482951217890527)
XLA Ops:
  6.5 26.4 %all_gather.3 = bf16[256,1024]{1,0:T(8,128)(2,1)S(1)} all-gather(bf16[256,128]{1,0:T(8,128)(2,1)} %param.8), channel_id=1, replica_groups=mesh['space'=64,'scen'=8] {'scen'}, dimensions={1}, use_global_device_ids=true | all-gather | bytes 589824 | tf_op jit(solution)/shard_map/all_gather | solution.py:105
  34.9 6.0 %collective-permute-start.1 = (bf16[63,1024]{1,0:T(8,128)(2,1)S(1)}, bf16[63,1024]{1,0:T(8,128)(2,1)S(1)}, u32[]{:S(2)}, u32[]{:S(2)}) collective-permute-start(bf16[63,1024]{1,0:T(8,128)(2,1)S(1)} %get-tuple-element.86), channel_id=1, source_target_pairs={{8,0},{16,8},{24,16},{32,24},{40,32},{48,40},{56,48},{64,56},{72,6... | collective-permute-start | bytes 387080 | tf_op jit(solution)/shard_map/ppermute | solution.py:20
  43.6 13.4 %while.5 = (s32[]{:T(128)}, bf16[2,255]{1,0:T(2,128)(2,1)S(1)}, s32[2,2]{1,0:T(2,128)S(1)}, bf16[2,63]{1,0:T(2,128)(2,1)S(1)}, s32[]{:T(128)}, /*index=5*/s32[2]{0:T(128)}) while((s32[]{:T(128)}, bf16[2,255]{1,0:T(2,128)(2,1)S(1)}, s32[2,2]{1,0:T(2,128)S(1)}, bf16[2,63]{1,0:T(2,128)(2,1)S(1)}, s32[]{:T(128)}, /*index=5*/s32[2]{0:T(128)}) %tuple.77), condition=%wide.while_cond.1, body=%wide.while_body.1.sunk | while | flops 74 | bytes 769 | solution.py:27
  44.2 2.7 %and_reduce_fusion.9 = pred[]{:T(512)} fusion(s32[2]{0:T(128)} %get-tuple-element.250, s32[1]{0:T(128)} %bitcast.121, s32[1]{0:T(128)} %bitcast.122), kind=kLoop, calls=%fused_computation.3.clone.1 | loop fusion | flops 9 | bytes 17 | tf_op jit(solution)/shard_map/vmap(vmap())/scatter
  50.9 2.7 %and_reduce_fusion.9 = pred[]{:T(512)} fusion(s32[2]{0:T(128)} %get-tuple-element.250, s32[1]{0:T(128)} %bitcast.121, s32[1]{0:T(128)} %bitcast.122), kind=kLoop, calls=%fused_computation.3.clone.1 | loop fusion | flops 9 | bytes 17 | tf_op jit(solution)/shard_map/vmap(vmap())/scatter
  57.2 13.7 %while.6 = (s32[]{:T(128)}, bf16[2,385]{1,0:T(2,128)(2,1)S(1)}, s32[2,2]{1,0:T(2,128)S(1)}, bf16[2,63]{1,0:T(2,128)(2,1)S(1)}, s32[]{:T(128)}, /*index=5*/s32[2]{0:T(128)}) while((s32[]{:T(128)}, bf16[2,385]{1,0:T(2,128)(2,1)S(1)}, s32[2,2]{1,0:T(2,128)S(1)}, bf16[2,63]{1,0:T(2,128)(2,1)S(1)}, s32[]{:T(128)}, /*index=5*/s32[2]{0:T(128)}) %tuple.80), condition=%wide.while_cond.2, body=%wide.while_body.2.sunk | while | flops 74 | bytes 769 | solution.py:27
  57.8 2.7 %and_reduce_fusion.10 = pred[]{:T(512)} fusion(s32[2]{0:T(128)} %get-tuple-element.268, s32[1]{0:T(128)} %bitcast.125, s32[1]{0:T(128)} %bitcast.126), kind=kLoop, calls=%fused_computation.6.clone.1 | loop fusion | flops 9 | bytes 17 | tf_op jit(solution)/shard_map/vmap(vmap())/scatter
  64.6 2.7 %and_reduce_fusion.10 = pred[]{:T(512)} fusion(s32[2]{0:T(128)} %get-tuple-element.268, s32[1]{0:T(128)} %bitcast.125, s32[1]{0:T(128)} %bitcast.126), kind=kLoop, calls=%fused_computation.6.clone.1 | loop fusion | flops 9 | bytes 17 | tf_op jit(solution)/shard_map/vmap(vmap())/scatter
  70.9 13.5 %while.7 = (s32[]{:T(128)}, bf16[2,385]{1,0:T(2,128)(2,1)S(1)}, s32[2,2]{1,0:T(2,128)S(1)}, bf16[2,63]{1,0:T(2,128)(2,1)S(1)}, s32[]{:T(128)}, /*index=5*/s32[2]{0:T(128)}) while((s32[]{:T(128)}, bf16[2,385]{1,0:T(2,128)(2,1)S(1)}, s32[2,2]{1,0:T(2,128)S(1)}, bf16[2,63]{1,0:T(2,128)(2,1)S(1)}, s32[]{:T(128)}, /*index=5*/s32[2]{0:T(128)}) %tuple.89), condition=%wide.while_cond.3, body=%wide.while_body.3.sunk | while | flops 74 | bytes 769 | solution.py:27
  71.6 2.6 %and_reduce_fusion.11 = pred[]{:T(512)} fusion(s32[2]{0:T(128)} %get-tuple-element.286, s32[1]{0:T(128)} %bitcast.129, s32[1]{0:T(128)} %bitcast.130), kind=kLoop, calls=%fused_computation.9.clone.1 | loop fusion | flops 9 | bytes 17 | tf_op jit(solution)/shard_map/vmap(vmap())/scatter
  78.4 2.6 %and_reduce_fusion.11 = pred[]{:T(512)} fusion(s32[2]{0:T(128)} %get-tuple-element.286, s32[1]{0:T(128)} %bitcast.129, s32[1]{0:T(128)} %bitcast.130), kind=kLoop, calls=%fused_computation.9.clone.1 | loop fusion | flops 9 | bytes 17 | tf_op jit(solution)/shard_map/vmap(vmap())/scatter
  93.0 6.2 %collective-permute-start.3 = (bf16[2,63,1024]{1,2,0:T(8,128)(2,1)S(1)}, bf16[2,63,1024]{1,2,0:T(8,128)(2,1)}, u32[]{:S(2)}, u32[]{:S(2)}) collective-permute-start(bf16[2,63,1024]{1,2,0:T(8,128)(2,1)S(1)} %get-tuple-element.84), channel_id=1, source_target_pairs={{8,0},{16,8},{24,16},{32,24},{40,32},{48,40},{56,48},{64,56},{72,6... | collective-permute-start | bytes 774152 | tf_op jit(solution)/shard_map/ppermute | solution.py:20
  99.3 12.7 %while.4 = (s32[]{:T(128)}, bf16[2,255]{1,0:T(2,128)(2,1)S(1)}, s32[2,2]{1,0:T(2,128)S(1)}, bf16[2,63]{1,0:T(2,128)(2,1)S(1)}, s32[]{:T(128)}, /*index=5*/s32[2]{0:T(128)S(1)}) while((s32[]{:T(128)}, bf16[2,255]{1,0:T(2,128)(2,1)S(1)}, s32[2,2]{1,0:T(2,128)S(1)}, bf16[2,63]{1,0:T(2,128)(2,1)S(1)}, s32[]{:T(128)}, /*index=5*/s32[2]{0:T(128)S(1)}) %tuple.88), condition=%wide.while_cond, body=%wide.while_body.sunk | while | flops 74 | bytes 769 | solution.py:27
  100.0 2.0 %and_reduce_fusion.8 = pred[]{:T(512)} fusion(s32[2]{0:T(128)S(1)} %get-tuple-element.232, s32[1]{0:T(128)} %bitcast.117, s32[1]{0:T(128)} %bitcast.118), kind=kLoop, calls=%fused_computation.clone.1 | loop fusion | flops 9 | bytes 17 | tf_op jit(solution)/shard_map/vmap(vmap())/scatter
  102.0 2.0 %broadcast_select_fusion.8 = bf16[1,63]{1,0:T(2,128)(2,1)S(1)} fusion(pred[]{:T(512)} %and_reduce_fusion.8, bf16[2,63]{1,0:T(2,128)(2,1)S(1)} %get-tuple-element.230, s32[]{:T(128)} %get-tuple-element.221, bf16[2,255]{1,0:T(2,128)(2,1)S(1)} %get-tuple-element.222, s32[]{:T(128)} %bitcast.119, s32[]{:T(128)} %bitcast.120), kind=kLoop, calls=%fused_computation.1.clone.1 | loop fusion | flops 63 | bytes 391 | tf_op jit(solution)/shard_map/vmap(vmap())/scatter
  106.3 2.0 %and_reduce_fusion.8 = pred[]{:T(512)} fusion(s32[2]{0:T(128)S(1)} %get-tuple-element.232, s32[1]{0:T(128)} %bitcast.117, s32[1]{0:T(128)} %bitcast.118), kind=kLoop, calls=%fused_computation.clone.1 | loop fusion | flops 9 | bytes 17 | tf_op jit(solution)/shard_map/vmap(vmap())/scatter
  108.3 2.0 %broadcast_select_fusion.8 = bf16[1,63]{1,0:T(2,128)(2,1)S(1)} fusion(pred[]{:T(512)} %and_reduce_fusion.8, bf16[2,63]{1,0:T(2,128)(2,1)S(1)} %get-tuple-element.230, s32[]{:T(128)} %get-tuple-element.221, bf16[2,255]{1,0:T(2,128)(2,1)S(1)} %get-tuple-element.222, s32[]{:T(128)} %bitcast.119, s32[]{:T(128)} %bitcast.120), kind=kLoop, calls=%fused_computation.1.clone.1 | loop fusion | flops 63 | bytes 391 | tf_op jit(solution)/shard_map/vmap(vmap())/scatter
  114.8 2.2 %pad_maximum_fusion = bf16[2,382,1024]{1,2,0:T(8,128)(2,1)S(1)} fusion(bf16[2,63,1024]{1,2,0:T(8,128)(2,1)} %collective-permute-done.3, bf16[2,256,1024]{1,2,0:T(8,128)(2,1)S(1)} %fusion.3, bf16[2,63,1024]{1,2,0:T(8,128)(2,1)} %copy-done.3), kind=kLoop, calls=%fused_computation.26 | loop fusion | flops 4694016 | bytes 3129344 | tf_op jit(solution)/shard_map/concatenate | solution.py:21
  118.4 2.9 %copy.48 = bf16[2,382,8,128]{3,2,1,0:T(8,128)(2,1)} copy(bf16[2,382,8,128]{1,3,2,0:T(8,128)(2,1)} %bitcast.137) | data formatting | bytes 3129344 | tf_op jit(solution)/shard_map/reshape | solution.py:42
  123.4 3.7 %fusion.28 = f32[2,382,8,128]{3,2,1,0:T(8,128)} fusion(bf16[2,382,8,128]{3,2,1,0:T(8,128)(2,1)} %copy.48, bf16[2,128,384]{2,1,0:T(8,128)(2,1)S(1)} %bitcast.139), kind=kOutput, calls=%fused_computation.61 | convolution fusion | flops 200278016 | bytes 4759552 | tf_op jit(solution)/shard_map/srny,scy->srnc/dot_general | solution.py:46
  127.1 2.2 %fusion.27 = f32[2,382,8,128]{3,2,1,0:T(8,128)} fusion(bf16[2,382,8,128]{3,2,1,0:T(8,128)(2,1)S(1)} %copy-done.1, bf16[2,128,384]{2,1,0:T(8,128)(2,1)S(1)} %bitcast.140), kind=kOutput, calls=%fused_computation.58 | convolution fusion | flops 200278016 | bytes 4759552 | tf_op jit(solution)/shard_map/srny,scy->srnc/dot_general | solution.py:46
  130.6 4.7 %add_convert_fusion = bf16[2,382,8,128]{3,2,1,0:T(8,128)(2,1)} fusion(f32[2,382,8,128]{3,2,1,0:T(8,128)} %fusion.27, f32[2,382,8,128]{3,2,1,0:T(8,128)} %fusion.28, bf16[2,382,8,128]{3,2,1,0:T(8,128)(2,1)S(1)} %copy.49, bf16[2,128,384]{2,1,0:T(8,128)(2,1)S(1)} %bitcast.141), kind=kOutput, calls=%fused_computation.14 | convolution fusion | flops 202625024 | bytes 9453568 | tf_op jit(solution)/shard_map/srny,scy->srnc/dot_general | solution.py:46
  135.2 2.1 %copy.51 = bf16[2,382,8,128]{1,3,2,0:T(8,128)(2,1)S(1)} copy(bf16[2,382,8,128]{3,2,1,0:T(8,128)(2,1)} %add_convert_fusion) | data formatting | bytes 3129344 | tf_op jit(solution)/shard_map/convert_element_type | solution.py:111
  139.7 48.7 %reduce-scatter.4.cloned.1.call-done = bf16[128,256]{1,0:T(8,128)(2,1)} async-done(((bf16[1024,256]{1,0:T(8,128)(2,1)}), bf16[128,256]{1,0:T(8,128)(2,1)}) %reduce-scatter.4.cloned.1.call-update) | async-done | bytes 65552
  (112 shorter events, 53.6 us)
Async XLA Ops:
  6.5 34.5 %copy-start = (s32[16,2]{0,1:T(2,128)S(1)}, s32[16,2]{0,1:T(2,128)}, u32[]{:S(2)}) copy-start(s32[16,2]{0,1:T(2,128)} %param.11) | copy-start | bytes 388
  6.5 80.0 %copy-start.2 = (bf16[256,1024]{1,0:T(8,128)(2,1)S(1)}, bf16[256,1024]{1,0:T(8,128)(2,1)}, u32[]{:S(2)}) copy-start(bf16[256,1024]{1,0:T(8,128)(2,1)} %param.9) | copy-start | bytes 1572868
  6.5 181.8 %reduce-scatter.4.cloned.1.call-start = ((), (), s32[]{:S(2)}) async-start(), calls=%async_computation.1 | async-start | bytes 589824
  33.0 53.9 %collective-permute-start = (bf16[63,1024]{1,0:T(8,128)(2,1)S(1)}, bf16[63,1024]{1,0:T(8,128)(2,1)S(1)}, u32[]{:S(2)}, u32[]{:S(2)}) collective-permute-start(bf16[63,1024]{1,0:T(8,128)(2,1)S(1)} %get-tuple-element.85), channel_id=1, source_target_pairs={{0,8},{8,16},{16,24},{24,32},{32,40},{40,48},{48,56},{56,64},{64,7... | collective-permute-start | bytes 387080 | tf_op jit(solution)/shard_map/ppermute | solution.py:19
  34.9 52.4 %collective-permute-start.1 = (bf16[63,1024]{1,0:T(8,128)(2,1)S(1)}, bf16[63,1024]{1,0:T(8,128)(2,1)S(1)}, u32[]{:S(2)}, u32[]{:S(2)}) collective-permute-start(bf16[63,1024]{1,0:T(8,128)(2,1)S(1)} %get-tuple-element.86), channel_id=1, source_target_pairs={{8,0},{16,8},{24,16},{32,24},{40,32},{48,40},{56,48},{64,56},{72,6... | collective-permute-start | bytes 387080 | tf_op jit(solution)/shard_map/ppermute | solution.py:20
  70.9 15.8 %copy-start.7 = (f32[4]{0:T(128)S(1)}, f32[4]{0:T(128)}, u32[]{:S(2)}) copy-start(f32[4]{0:T(128)} %param.13) | copy-start | bytes 52
  90.1 9.2 %copy-start.6 = (s32[2]{0:T(128)S(1)}, s32[2]{0:T(128)}, u32[]{:S(2)}) copy-start(s32[2]{0:T(128)} %get-tuple-element.297) | copy-start | bytes 28
  91.1 22.8 %collective-permute-start.2 = (bf16[2,63,1024]{1,2,0:T(8,128)(2,1)}, bf16[2,63,1024]{1,2,0:T(8,128)(2,1)S(1)}, u32[]{:S(2)}, u32[]{:S(2)}) collective-permute-start(bf16[2,63,1024]{1,2,0:T(8,128)(2,1)} %get-tuple-element.83), channel_id=1, source_target_pairs={{0,8},{8,16},{16,24},{24,32},{32,40},{40,48},{48,56},{56,64},{64,7... | collective-permute-start | bytes 774152 | tf_op jit(solution)/shard_map/ppermute | solution.py:19
  93.0 21.7 %collective-permute-start.3 = (bf16[2,63,1024]{1,2,0:T(8,128)(2,1)S(1)}, bf16[2,63,1024]{1,2,0:T(8,128)(2,1)}, u32[]{:S(2)}, u32[]{:S(2)}) collective-permute-start(bf16[2,63,1024]{1,2,0:T(8,128)(2,1)S(1)} %get-tuple-element.84), channel_id=1, source_target_pairs={{8,0},{16,8},{24,16},{32,24},{40,32},{48,40},{56,48},{64,56},{72,6... | collective-permute-start | bytes 774152 | tf_op jit(solution)/shard_map/ppermute | solution.py:20
  114.0 0.8 copy-start.3
  123.4 3.7 %copy-start.1 = (bf16[2,382,8,128]{3,2,1,0:T(8,128)(2,1)S(1)}, bf16[2,382,8,128]{3,2,1,0:T(8,128)(2,1)}, u32[]{:S(2)}) copy-start(bf16[2,382,8,128]{3,2,1,0:T(8,128)(2,1)} %copy.50) | copy-start | bytes 4694020
  138.3 51.0 %copy-start.4 = (bf16[256,128]{1,0:T(8,128)(2,1)S(1)}, bf16[256,128]{1,0:T(8,128)(2,1)}, u32[]{:S(2)}) copy-start(bf16[256,128]{1,0:T(8,128)(2,1)} %param.8) | copy-start | bytes 196612
  138.3 51.0 %copy-start.5 = (s32[256,128]{1,0:T(8,128)S(1)}, s32[256,128]{1,0:T(8,128)}, u32[]{:S(2)}) copy-start(s32[256,128]{1,0:T(8,128)} %param.10) | copy-start | bytes 393220
Sparse Core Ops, SparseCore 0:
  139.8 48.5 reduce-scatter.3
where the time goes:
time: 198 us; the launch traced here: 197 us
  waiting for transfers between devices  48.7 us (25%)
  other arithmetic  41.2 us (21%)
  local copies, waits for them, and re-layouts  36.8 us (19%)
  blocking collectives  26.4 us (13%)
  starting transfers between devices  16.1 us (8%)
  between operations  13.8 us (7%)
  matrix products  13.6 us (7%)
    unnamed x2, waiting for transfers between devices  48.7 us
    scatter x16, other arithmetic  35.7 us
    all_gather x1, blocking collectives, shards(): full_map = lax.all_gather(dwell_map, 'scen', axis=1, tiled=True)  26.4 us
    scatter x24, local copies, waits for them, and re-layouts  17.4 us
    ppermute x2, starting transfers between devices, extended(): after = lax.ppermute(first, axis, down)  12.3 us
    dot_general x6, matrix products, column_pass(): jnp.einsum('srny,scy->srnc', view, part_mat, preferred_element_type=jnp.f...  12 us
    reshape x3, local copies, waits for them, and re-layouts, column_pass(): padded[:, :, piece * col_block:piece * col_block + col_total]  6.16 us
  transfers between devices with their start and end apart: 5, of which 1 were waited for; matrix products, arithmetic and copies ran while one was open for 31% of the time, Pallas kernels for 0%

commit v1 on v0

--- a/solution.py
+++ b/solution.py
@@ -2,6 +2,7 @@
 import jax.numpy as jnp
 from jax import lax
 from jax.sharding import PartitionSpec as P
+from jax.lax import all_to_all, axis_size
 
 S_DEV = 2
 KTAPS = 63
@@ -102,7 +103,20 @@
     my_col_taps = jnp.sum(
         onehot[:, :, None] * col_kernels.astype(jnp.float32)[None], axis=1
     ).astype(jnp.bfloat16)
-    full_map = lax.all_gather(dwell_map, "scen", axis=1, tiled=True)
+
+    def _finish_spot(inp):
+        even = jnp.concatenate(
+            all_to_all(
+                jnp.stack(tuple((inp for _ in range(axis_size("scen")))), axis=0),
+                axis_name="scen",
+                split_axis=0,
+                concat_axis=0,
+            ),
+            axis=1,
+        )
+        return even
+
+    full_map = _finish_spot(dwell_map)
     rim_rows = extended(full_map, (("space", 0),), halo_rows)
     forward = row_pass(rim_rows, my_row_taps, -radius - shift_rows, tile_rows).astype(jnp.bfloat16)
     removal = my_rates[:, None, None] * column_pass(forward, my_col_taps, -radius - shift_cols)

time: 198 us -> 183 us (0.924)
  the two profiles are of different devices: /device:TPU:32 before, /device:TPU:4 now
where the time goes in v1:
time: 183 us; the launch traced here: 182 us
  waiting for transfers between devices  55 us (30%)
  other arithmetic  40.8 us (22%)
  local copies, waits for them, and re-layouts  38.8 us (21%)
  starting transfers between devices  19.7 us (11%)
  between operations  13.9 us (8%)
  matrix products  13.6 us (7%)
    unnamed x2, waiting for transfers between devices  53 us
    scatter x16, other arithmetic  35.3 us
    scatter x24, local copies, waits for them, and re-layouts  17.3 us
    dot_general x6, matrix products, column_pass(): jnp.einsum('srny,scy->srnc', view, part_mat, preferred_element_type=jnp.f...  12 us
    ppermute x2, starting transfers between devices, extended(): after = lax.ppermute(first, axis, down)  7.33 us
    ppermute x2, starting transfers between devices, extended(): before = lax.ppermute(last, axis, up)  7.1 us
    reshape x3, local copies, waits for them, and re-layouts, column_pass(): padded[:, :, piece * col_block:piece * col_block + col_total]  6.15 us
    all_to_all x1, starting transfers between devices, _finish_spot(): all_to_all(jnp.stack(tuple((inp for _ in range(axis_size('scen')))), axis...  5.24 us
  transfers between devices with their start and end apart: 6, of which 3 were waited for; matrix products, arithmetic and copies ran while one was open for 33% of the time, Pallas kernels for 0%

profile of v1, /device:TPU:4, one launch (start us, length us, event | category | flops | bytes accessed | tf_op | source)
XLA Modules:
  0.0 182.0 jit_solution(2148863904584651767)
XLA Ops:
  8.3 5.2 %all-to-all-start = ((bf16[8,256,128]{2,1,0:T(8,128)(2,1)}), bf16[8,256,128]{2,1,0:T(8,128)(2,1)S(1)}, u32[]{:S(2)}, u32[]{:S(2)}) async-start(bf16[8,256,128]{2,1,0:T(8,128)(2,1)} %stack.2), calls=%async_computation | async-start | bytes 1048576 | tf_op jit(solution)/shard_map/all_to_all | solution.py:109
  16.2 13.5 %while.5 = (s32[]{:T(128)}, bf16[2,255]{1,0:T(2,128)(2,1)S(1)}, s32[2,2]{1,0:T(2,128)S(1)}, bf16[2,63]{1,0:T(2,128)(2,1)S(1)}, s32[]{:T(128)}, /*index=5*/s32[2]{0:T(128)}) while((s32[]{:T(128)}, bf16[2,255]{1,0:T(2,128)(2,1)S(1)}, s32[2,2]{1,0:T(2,128)S(1)}, bf16[2,63]{1,0:T(2,128)(2,1)S(1)}, s32[]{:T(128)}, /*index=5*/s32[2]{0:T(128)}) %tuple.77), condition=%wide.while_cond.1, body=%wide.while_body.1.sunk | while | flops 74 | bytes 769 | solution.py:28
  16.8 2.7 %and_reduce_fusion.9 = pred[]{:T(512)} fusion(s32[2]{0:T(128)} %get-tuple-element.250, s32[1]{0:T(128)} %bitcast.133, s32[1]{0:T(128)} %bitcast.134), kind=kLoop, calls=%fused_computation.3.clone.1 | loop fusion | flops 9 | bytes 17 | tf_op jit(solution)/shard_map/vmap(vmap())/scatter
  23.5 2.7 %and_reduce_fusion.9 = pred[]{:T(512)} fusion(s32[2]{0:T(128)} %get-tuple-element.250, s32[1]{0:T(128)} %bitcast.133, s32[1]{0:T(128)} %bitcast.134), kind=kLoop, calls=%fused_computation.3.clone.1 | loop fusion | flops 9 | bytes 17 | tf_op jit(solution)/shard_map/vmap(vmap())/scatter
  29.8 13.5 %while.6 = (s32[]{:T(128)}, bf16[2,385]{1,0:T(2,128)(2,1)S(1)}, s32[2,2]{1,0:T(2,128)S(1)}, bf16[2,63]{1,0:T(2,128)(2,1)S(1)}, s32[]{:T(128)}, /*index=5*/s32[2]{0:T(128)}) while((s32[]{:T(128)}, bf16[2,385]{1,0:T(2,128)(2,1)S(1)}, s32[2,2]{1,0:T(2,128)S(1)}, bf16[2,63]{1,0:T(2,128)(2,1)S(1)}, s32[]{:T(128)}, /*index=5*/s32[2]{0:T(128)}) %tuple.80), condition=%wide.while_cond.2, body=%wide.while_body.2.sunk | while | flops 74 | bytes 769 | solution.py:28
  30.4 2.6 %and_reduce_fusion.10 = pred[]{:T(512)} fusion(s32[2]{0:T(128)} %get-tuple-element.268, s32[1]{0:T(128)} %bitcast.137, s32[1]{0:T(128)} %bitcast.138), kind=kLoop, calls=%fused_computation.6.clone.1 | loop fusion | flops 9 | bytes 17 | tf_op jit(solution)/shard_map/vmap(vmap())/scatter
  37.1 2.6 %and_reduce_fusion.10 = pred[]{:T(512)} fusion(s32[2]{0:T(128)} %get-tuple-element.268, s32[1]{0:T(128)} %bitcast.137, s32[1]{0:T(128)} %bitcast.138), kind=kLoop, calls=%fused_computation.6.clone.1 | loop fusion | flops 9 | bytes 17 | tf_op jit(solution)/shard_map/vmap(vmap())/scatter
  43.3 13.6 %while.7 = (s32[]{:T(128)}, bf16[2,385]{1,0:T(2,128)(2,1)S(1)}, s32[2,2]{1,0:T(2,128)S(1)}, bf16[2,63]{1,0:T(2,128)(2,1)S(1)}, s32[]{:T(128)}, /*index=5*/s32[2]{0:T(128)}) while((s32[]{:T(128)}, bf16[2,385]{1,0:T(2,128)(2,1)S(1)}, s32[2,2]{1,0:T(2,128)S(1)}, bf16[2,63]{1,0:T(2,128)(2,1)S(1)}, s32[]{:T(128)}, /*index=5*/s32[2]{0:T(128)}) %tuple.89), condition=%wide.while_cond.3, body=%wide.while_body.3.sunk | while | flops 74 | bytes 769 | solution.py:28
  43.9 2.6 %and_reduce_fusion.11 = pred[]{:T(512)} fusion(s32[2]{0:T(128)} %get-tuple-element.286, s32[1]{0:T(128)} %bitcast.141, s32[1]{0:T(128)} %bitcast.142), kind=kLoop, calls=%fused_computation.9.clone.1 | loop fusion | flops 9 | bytes 17 | tf_op jit(solution)/shard_map/vmap(vmap())/scatter
  50.7 2.6 %and_reduce_fusion.11 = pred[]{:T(512)} fusion(s32[2]{0:T(128)} %get-tuple-element.286, s32[1]{0:T(128)} %bitcast.141, s32[1]{0:T(128)} %bitcast.142), kind=kLoop, calls=%fused_computation.9.clone.1 | loop fusion | flops 9 | bytes 17 | tf_op jit(solution)/shard_map/vmap(vmap())/scatter
  61.6 5.1 %collective-permute-start.1 = (bf16[63,1024]{1,0:T(8,128)(2,1)S(1)}, bf16[63,1024]{1,0:T(8,128)(2,1)S(1)}, u32[]{:S(2)}, u32[]{:S(2)}) collective-permute-start(bf16[63,1024]{1,0:T(8,128)(2,1)S(1)} %bitcast.163), channel_id=1, source_target_pairs={{8,0},{16,8},{24,16},{32,24},{40,32},{48,40},{56,48},{64,56},{72,6... | collective-permute-start | bytes 387080 | tf_op jit(solution)/shard_map/ppermute | solution.py:21
  73.0 5.2 %collective-permute-start.2 = (bf16[2,63,1024]{1,2,0:T(8,128)(2,1)}, bf16[2,63,1024]{1,2,0:T(8,128)(2,1)S(1)}, u32[]{:S(2)}, u32[]{:S(2)}) collective-permute-start(bf16[2,63,1024]{1,2,0:T(8,128)(2,1)} %get-tuple-element.83), channel_id=1, source_target_pairs={{0,8},{8,16},{16,24},{24,32},{32,40},{40,48},{48,56},{56,64},{64,7... | collective-permute-start | bytes 774152 | tf_op jit(solution)/shard_map/ppermute | solution.py:20
  78.2 2.2 %collective-permute-start.3 = (bf16[2,63,1024]{1,2,0:T(8,128)(2,1)S(1)}, bf16[2,63,1024]{1,2,0:T(8,128)(2,1)}, u32[]{:S(2)}, u32[]{:S(2)}) collective-permute-start(bf16[2,63,1024]{1,2,0:T(8,128)(2,1)S(1)} %get-tuple-element.84), channel_id=1, source_target_pairs={{8,0},{16,8},{24,16},{32,24},{40,32},{48,40},{56,48},{64,56},{72,6... | collective-permute-start | bytes 774152 | tf_op jit(solution)/shard_map/ppermute | solution.py:21
  80.4 12.3 %while.4 = (s32[]{:T(128)}, bf16[2,255]{1,0:T(2,128)(2,1)S(1)}, s32[2,2]{1,0:T(2,128)S(1)}, bf16[2,63]{1,0:T(2,128)(2,1)S(1)}, s32[]{:T(128)}, /*index=5*/s32[2]{0:T(128)S(1)}) while((s32[]{:T(128)}, bf16[2,255]{1,0:T(2,128)(2,1)S(1)}, s32[2,2]{1,0:T(2,128)S(1)}, bf16[2,63]{1,0:T(2,128)(2,1)S(1)}, s32[]{:T(128)}, /*index=5*/s32[2]{0:T(128)S(1)}) %tuple.88), condition=%wide.while_cond, body=%wide.while_body.sunk | while | flops 74 | bytes 769 | solution.py:28
  81.1 2.0 %and_reduce_fusion.8 = pred[]{:T(512)} fusion(s32[2]{0:T(128)S(1)} %get-tuple-element.232, s32[1]{0:T(128)} %bitcast.129, s32[1]{0:T(128)} %bitcast.130), kind=kLoop, calls=%fused_computation.clone.1 | loop fusion | flops 9 | bytes 17 | tf_op jit(solution)/shard_map/vmap(vmap())/scatter
  87.2 2.0 %and_reduce_fusion.8 = pred[]{:T(512)} fusion(s32[2]{0:T(128)S(1)} %get-tuple-element.232, s32[1]{0:T(128)} %bitcast.129, s32[1]{0:T(128)} %bitcast.130), kind=kLoop, calls=%fused_computation.clone.1 | loop fusion | flops 9 | bytes 17 | tf_op jit(solution)/shard_map/vmap(vmap())/scatter
  95.6 2.2 %pad_maximum_fusion = bf16[2,382,1024]{1,2,0:T(8,128)(2,1)S(1)} fusion(bf16[2,63,1024]{1,2,0:T(8,128)(2,1)} %collective-permute-done.3, bf16[2,256,1024]{1,2,0:T(8,128)(2,1)S(1)} %fusion.3, bf16[2,63,1024]{1,2,0:T(8,128)(2,1)} %copy-done.3), kind=kLoop, calls=%fused_computation.26 | loop fusion | flops 4694016 | bytes 3129344 | tf_op jit(solution)/shard_map/concatenate | solution.py:22
  99.2 2.9 %copy.54 = bf16[2,382,8,128]{3,2,1,0:T(8,128)(2,1)} copy(bf16[2,382,8,128]{1,3,2,0:T(8,128)(2,1)} %bitcast.149) | data formatting | bytes 3129344 | tf_op jit(solution)/shard_map/reshape | solution.py:43
  102.2 2.0 %copy.56 = bf16[2,382,8,128]{3,2,1,0:T(8,128)(2,1)} copy(bf16[2,382,8,128]{1,3,2,0:T(8,128)(2,1)S(1)} %bitcast.148) | data formatting | bytes 3129344 | tf_op jit(solution)/shard_map/reshape | solution.py:43
  104.2 3.7 %fusion.28 = f32[2,382,8,128]{3,2,1,0:T(8,128)} fusion(bf16[2,382,8,128]{3,2,1,0:T(8,128)(2,1)} %copy.54, bf16[2,128,384]{2,1,0:T(8,128)(2,1)S(1)} %bitcast.152), kind=kOutput, calls=%fused_computation.62 | convolution fusion | flops 200278016 | bytes 4759552 | tf_op jit(solution)/shard_map/srny,scy->srnc/dot_general | solution.py:47
  107.9 2.2 %fusion.27 = f32[2,382,8,128]{3,2,1,0:T(8,128)} fusion(bf16[2,382,8,128]{3,2,1,0:T(8,128)(2,1)S(1)} %copy-done.1, bf16[2,128,384]{2,1,0:T(8,128)(2,1)S(1)} %bitcast.153), kind=kOutput, calls=%fused_computation.59 | convolution fusion | flops 200278016 | bytes 4759552 | tf_op jit(solution)/shard_map/srny,scy->srnc/dot_general | solution.py:47
  111.4 4.7 %add_convert_fusion = bf16[2,382,8,128]{3,2,1,0:T(8,128)(2,1)} fusion(f32[2,382,8,128]{3,2,1,0:T(8,128)} %fusion.27, f32[2,382,8,128]{3,2,1,0:T(8,128)} %fusion.28, bf16[2,382,8,128]{3,2,1,0:T(8,128)(2,1)S(1)} %copy.55, bf16[2,128,384]{2,1,0:T(8,128)(2,1)S(1)} %bitcast.154), kind=kOutput, calls=%fused_computation.14 | convolution fusion | flops 202625024 | bytes 9453568 | tf_op jit(solution)/shard_map/srny,scy->srnc/dot_general | solution.py:47
  116.0 2.1 %copy.57 = bf16[2,382,8,128]{1,3,2,0:T(8,128)(2,1)S(1)} copy(bf16[2,382,8,128]{3,2,1,0:T(8,128)(2,1)} %add_convert_fusion) | data formatting | bytes 3129344 | tf_op jit(solution)/shard_map/convert_element_type | solution.py:125
  120.5 53.0 %reduce-scatter.4.cloned.1.call-done = bf16[128,256]{1,0:T(8,128)(2,1)} async-done(((bf16[1024,256]{1,0:T(8,128)(2,1)}), bf16[128,256]{1,0:T(8,128)(2,1)}) %reduce-scatter.4.cloned.1.call-update) | async-done | bytes 65552
  (121 shorter events, 57.5 us)
Async XLA Ops:
  6.5 7.0 %copy-start = (s32[16,2]{0,1:T(2,128)S(1)}, s32[16,2]{0,1:T(2,128)}, u32[]{:S(2)}) copy-start(s32[16,2]{0,1:T(2,128)} %param.11) | copy-start | bytes 388
  8.3 50.7 %copy-start.2 = (bf16[256,1024]{1,0:T(8,128)(2,1)S(1)}, bf16[256,1024]{1,0:T(8,128)(2,1)}, u32[]{:S(2)}) copy-start(bf16[256,1024]{1,0:T(8,128)(2,1)} %param.9) | copy-start | bytes 1572868
  8.3 51.1 %all-to-all-start = ((bf16[8,256,128]{2,1,0:T(8,128)(2,1)}), bf16[8,256,128]{2,1,0:T(8,128)(2,1)S(1)}, u32[]{:S(2)}, u32[]{:S(2)}) async-start(bf16[8,256,128]{2,1,0:T(8,128)(2,1)} %stack.2), calls=%async_computation | async-start | bytes 1048576 | tf_op jit(solution)/shard_map/all_to_all | solution.py:109
  13.5 160.0 %reduce-scatter.4.cloned.1.call-start = ((), (), s32[]{:S(2)}) async-start(), calls=%async_computation.2 | async-start | bytes 589824
  43.2 15.9 %copy-start.7 = (f32[4]{0:T(128)S(1)}, f32[4]{0:T(128)}, u32[]{:S(2)}) copy-start(f32[4]{0:T(128)} %param.13) | copy-start | bytes 52
  59.5 7.8 %collective-permute-start = (bf16[63,1024]{1,0:T(8,128)(2,1)S(1)}, bf16[63,1024]{1,0:T(8,128)(2,1)S(1)}, u32[]{:S(2)}, u32[]{:S(2)}) collective-permute-start(bf16[63,1024]{1,0:T(8,128)(2,1)S(1)} %bitcast.162), channel_id=1, source_target_pairs={{0,8},{8,16},{16,24},{24,32},{32,40},{40,48},{48,56},{56,64},{64,7... | collective-permute-start | bytes 387080 | tf_op jit(solution)/shard_map/ppermute | solution.py:20
  61.6 7.7 %collective-permute-start.1 = (bf16[63,1024]{1,0:T(8,128)(2,1)S(1)}, bf16[63,1024]{1,0:T(8,128)(2,1)S(1)}, u32[]{:S(2)}, u32[]{:S(2)}) collective-permute-start(bf16[63,1024]{1,0:T(8,128)(2,1)S(1)} %bitcast.163), channel_id=1, source_target_pairs={{8,0},{16,8},{24,16},{32,24},{40,32},{48,40},{56,48},{64,56},{72,6... | collective-permute-start | bytes 387080 | tf_op jit(solution)/shard_map/ppermute | solution.py:21
  72.0 8.5 %copy-start.6 = (s32[2]{0:T(128)S(1)}, s32[2]{0:T(128)}, u32[]{:S(2)}) copy-start(s32[2]{0:T(128)} %get-tuple-element.298) | copy-start | bytes 28
  73.0 21.7 %collective-permute-start.2 = (bf16[2,63,1024]{1,2,0:T(8,128)(2,1)}, bf16[2,63,1024]{1,2,0:T(8,128)(2,1)S(1)}, u32[]{:S(2)}, u32[]{:S(2)}) collective-permute-start(bf16[2,63,1024]{1,2,0:T(8,128)(2,1)} %get-tuple-element.83), channel_id=1, source_target_pairs={{0,8},{8,16},{16,24},{24,32},{32,40},{40,48},{48,56},{56,64},{64,7... | collective-permute-start | bytes 774152 | tf_op jit(solution)/shard_map/ppermute | solution.py:20
  78.2 17.4 %collective-permute-start.3 = (bf16[2,63,1024]{1,2,0:T(8,128)(2,1)S(1)}, bf16[2,63,1024]{1,2,0:T(8,128)(2,1)}, u32[]{:S(2)}, u32[]{:S(2)}) collective-permute-start(bf16[2,63,1024]{1,2,0:T(8,128)(2,1)S(1)} %get-tuple-element.84), channel_id=1, source_target_pairs={{8,0},{16,8},{24,16},{32,24},{40,32},{48,40},{56,48},{64,56},{72,6... | collective-permute-start | bytes 774152 | tf_op jit(solution)/shard_map/ppermute | solution.py:21
  94.8 0.8 copy-start.3
  104.2 3.7 %copy-start.1 = (bf16[2,382,8,128]{3,2,1,0:T(8,128)(2,1)S(1)}, bf16[2,382,8,128]{3,2,1,0:T(8,128)(2,1)}, u32[]{:S(2)}) copy-start(bf16[2,382,8,128]{3,2,1,0:T(8,128)(2,1)} %copy.56) | copy-start | bytes 4694020
  119.1 55.3 %copy-start.4 = (bf16[256,128]{1,0:T(8,128)(2,1)S(1)}, bf16[256,128]{1,0:T(8,128)(2,1)}, u32[]{:S(2)}) copy-start(bf16[256,128]{1,0:T(8,128)(2,1)} %param.8) | copy-start | bytes 196612
  119.1 55.3 %copy-start.5 = (s32[256,128]{1,0:T(8,128)S(1)}, s32[256,128]{1,0:T(8,128)}, u32[]{:S(2)}) copy-start(s32[256,128]{1,0:T(8,128)} %param.10) | copy-start | bytes 393220
Sparse Core Ops, SparseCore 0:
  120.6 52.8 reduce-scatter.3
